TPU v7x, 128 devices: a whole 4x4x4 slice. The times are simulated.
128 devices in a mesh: slab: 16 (over x, z), energy: 8 (over y, core).
Axes of the slice: x: 4, y: 4, z: 4, core: 2. Of those that a mesh axis runs over, the one named last changes fastest.
Arguments:
- green_lesser: bfloat16 [2, 16, 64, 256, 256], P(None, 'energy', 'slab'), may hold values from -4 to 4
- screened_lesser: bfloat16 [2, 16, 64, 256, 256], P(None, 'energy', 'slab'), may hold values from -4 to 4
- green_retarded: bfloat16 [2, 16, 64, 256, 256], P(None, 'energy', 'slab'), may hold values from -1 to 1
- coupling: bfloat16 [2, 64, 256, 256], P(None, 'slab'), may hold values from -1 to 1
Outputs:
- connected_lesser: float32 [2, 16, 64, 256, 256], P(None, 'energy', 'slab')
All inputs are finite; a program needn't handle non-finite values.
Results may differ from a plain program's by a relative error of at most 0.004.
Values may be sent and summed in bfloat16 or wider, within the bound.
A program may use at most 128 MiB of HBM per device.

v0:
```python
import jax
import jax.numpy as jnp
from jax import lax
from jax.sharding import PartitionSpec as P


def from_behind(x, axis, by):
    count = lax.axis_size(axis)
    pairs = [(i, i + by) for i in range(count) if 0 <= i + by < count]
    return lax.ppermute(x, axis, pairs)


def convolve_energy(green, screen):
    points = green.shape[1]
    middle = points // 2
    widths = [(0, 0)] * green.ndim
    widths[1] = (points, points)
    padded = jnp.pad(green.astype(jnp.float32), widths)
    screen_wide = screen.astype(jnp.float32)

    def add_offset(offset, totals):
        start = (points + middle - offset).astype(jnp.int32)
        shifted = lax.dynamic_slice_in_dim(padded, start, points, 1)
        weight = lax.dynamic_slice_in_dim(screen_wide, offset.astype(jnp.int32), 1, 1)
        real_part = totals[0] + shifted[0] * weight[0] - shifted[1] * weight[1]
        imag_part = totals[1] + shifted[0] * weight[1] + shifted[1] * weight[0]
        return (real_part, imag_part)

    blank_sum = jnp.zeros(green.shape[1:], jnp.float32)
    totals = lax.fori_loop(0, points, add_offset, (blank_sum, blank_sum))
    return jnp.stack([-totals[1] / points, totals[0] / points]).astype(jnp.bfloat16)


def precise(first, second):
    return jnp.einsum(
        "eij,ejk->eik",
        first,
        second,
        precision=lax.Precision.HIGHEST,
        preferred_element_type=jnp.float32,
    )


def precise_adjoint(first, second):
    return jnp.einsum(
        "eij,ekj->eik",
        first,
        second,
        precision=lax.Precision.HIGHEST,
        preferred_element_type=jnp.float32,
    )


def product(left, right):
    real_part = precise(left[0], right[0]) - precise(left[1], right[1])
    imag_part = precise(left[0], right[1]) + precise(left[1], right[0])
    return (real_part, imag_part)


def congruence(kernel, state, source):
    inner = product(kernel, state)
    outer_re = precise_adjoint(inner[0], kernel[0]) + precise_adjoint(inner[1], kernel[1])
    outer_im = precise_adjoint(inner[1], kernel[0]) - precise_adjoint(inner[0], kernel[1])
    return (outer_re + source[0], outer_im + source[1])


def lowprod(form, first, second):
    return jnp.einsum(form, first, second, preferred_element_type=jnp.float32)


def select_slab(pair, index):
    return (pair[0][:, index], pair[1][:, index])


def per_device(green_lesser, screened_lesser, green_retarded, coupling):
    sigma_rows = convolve_energy(
        lax.all_to_all(green_lesser, "energy", split_axis=3, concat_axis=1, tiled=True),
        lax.all_to_all(screened_lesser, "energy", split_axis=3, concat_axis=1, tiled=True),
    )
    sigma = lax.all_to_all(sigma_rows, "energy", split_axis=1, concat_axis=3, tiled=True)
    green_re = green_retarded[0]
    green_im = green_retarded[1]
    kernel_re = lowprod("esij,sjk->esik", green_re, coupling[0]) - lowprod(
        "esij,sjk->esik", green_im, coupling[1]
    )
    kernel_im = lowprod("esij,sjk->esik", green_re, coupling[1]) + lowprod(
        "esij,sjk->esik", green_im, coupling[0]
    )
    mixed_re = (
        lowprod("esij,esjk->esik", green_re, sigma[0])
        - lowprod("esij,esjk->esik", green_im, sigma[1])
    ).astype(jnp.bfloat16)
    mixed_im = (
        lowprod("esij,esjk->esik", green_re, sigma[1])
        + lowprod("esij,esjk->esik", green_im, sigma[0])
    ).astype(jnp.bfloat16)
    source_re = lowprod("esij,eskj->esik", mixed_re, green_re) + lowprod(
        "esij,eskj->esik", mixed_im, green_im
    )
    source_im = lowprod("esij,eskj->esik", mixed_im, green_re) - lowprod(
        "esij,eskj->esik", mixed_re, green_im
    )
    kernels = (kernel_re, kernel_im)
    sources = (source_re, source_im)
    slab_count = green_retarded.shape[2]
    block_shape = (green_retarded.shape[1], green_retarded.shape[3], green_retarded.shape[4])
    total_map = select_slab(kernels, 0)
    total_add = select_slab(sources, 0)
    for index in range(1, slab_count):
        total_add = congruence(select_slab(kernels, index), total_add, select_slab(sources, index))
        total_map = product(select_slab(kernels, index), total_map)

    def advance(turn, carried):
        applied = congruence(total_map, (carried[0], carried[1]), total_add)
        return from_behind(jnp.stack(applied), "slab", 1)

    carried = lax.fori_loop(
        0, lax.axis_size("slab") - 1, advance, jnp.zeros((2,) + block_shape, jnp.float32)
    )
    incoming = (carried[0], carried[1])
    state = incoming
    outputs = []
    for index in range(slab_count):
        state = congruence(select_slab(kernels, index), state, select_slab(sources, index))
        outputs.append(jnp.stack(state))
    return jnp.stack(outputs, axis=2)


def solution(mesh):
    placed = (
        P(None, "energy", "slab", None, None),
        P(None, "energy", "slab", None, None),
        P(None, "energy", "slab", None, None),
        P(None, "slab", None, None),
    )
    return jax.shard_map(
        per_device,
        mesh=mesh,
        in_specs=placed,
        out_specs=P(None, "energy", "slab", None, None),
        check_vma=False,
    )
```

profile of v0, /device:TPU:22, one launch (start us, length us, event | category | flops | bytes accessed | tf_op | source)
XLA Modules:
  0.0 819.1 jit_solution(10798756902314262669)
XLA Ops:
  0.0 4.5 copy.324
  4.5 4.8 all-to-all-start
  9.3 4.7 copy.326
  20.3 13.1 %all-to-all-done = bf16[2,2,4,256,256]{4,2,1,0,3:T(4,128)(2,1)} async-done(((bf16[2,2,4,256,256]{4,2,1,0,3:T(4,128)(2,1)}), bf16[2,2,4,256,256]{4,2,1,0,3:T(4,128)(2,1)}, u32[]{:S(2)}, u32[]{:S(2)}) %all-to-all-start) | async-done | bytes 2097184 | tf_op jit(solution)/shard_map/all_to_all | solution.py:77
  33.5 7.9 all-to-all-start.1
  41.4 2.3 add_bitcast_fusion
  45.8 1.9 fusion.90
  49.6 2.3 copy.325
  51.9 6.0 pad_convert_fusion
  58.0 7.5 all-to-all-done.1
  65.4 2.8 convert_bitcast_fusion
  68.3 4.4 copy.327
  72.7 126.0 %while.29 = (s32[]{:T(128)}, f32[16,4,32,256]{3,2,1,0:T(8,128)}, f32[16,4,32,256]{3,2,1,0:T(8,128)}, f32[2,48,4,32,256]{4,3,2,1,0:T(8,128)}, f32[2,16,4,32,256]{...) while((s32[]{:T(128)}, f32[16,4,32,256]{3,2,1,0:T(8,128)}, ...), condition=%wide.region_1.2_spmd.clone, body=%wide.region_0.1_spmd.clone.sunk | while | flops 5242888 | bytes 13369529 | solution.py:30
  73.7 5.7 fusion.227
  80.4 7.0 fusion.227
  88.4 7.0 fusion.227
  96.3 7.0 fusion.227
  104.3 7.0 fusion.227
  112.2 7.0 fusion.227
  120.2 7.0 fusion.227
  128.1 7.0 fusion.227
  136.1 7.0 fusion.227
  144.0 7.0 fusion.227
  152.0 7.0 fusion.227
  159.9 7.0 fusion.227
  167.9 7.0 fusion.227
  175.8 7.0 fusion.227
  183.8 7.0 fusion.227
  191.7 7.0 fusion.227
  198.7 2.9 fusion.32
  203.1 7.5 all-to-all-start.2
  210.6 2.1 fusion.91
  212.7 2.6 convolution_add_fusion.18
  220.6 14.0 %all-to-all-done.2 = bf16[2,16,4,32,256]{4,3,2,0,1:T(8,128)(2,1)} async-done(((bf16[2,16,4,32,256]{4,3,2,0,1:T(8,128)(2,1)}), bf16[2,16,4,32,256]{4,3,2,0,1:T(8,128)(2,1)}, u32[]{:S(2)}, u32[]{:S(2)}) %all-to-all-start.2) | async-done | bytes 2097184 | tf_op jit(solution)/shard_map/all_to_all | solution.py:80
  268.1 515.1 %while.28 = (s32[]{:T(128)}, f32[2,2,256,256]{3,2,1,0:T(8,128)}, f32[2,256,256]{2,1,0:T(8,128)S(1)}, f32[2,256,256]{2,1,0:T(8,128)S(1)}, f32[2,256,256]{2,1,0:T(8,128)}, /*index=5*/f32[2,256,256]{2,1,0:T(8,128)}, s32[]{:T(128)}) while((s32[]{:T(128)}, f32[2,2,256,256]{3,2,1,0:T(8,128)}, f32[2,256,256]{2,1,0:T(8,128)S(1)}, ...), condition=%wide.region_3.4_spmd, body=%wide.region_2.3_spmd.sunk | while | flops 3222274048 | bytes 26214572 | solution.py:117
  278.7 3.8 collective-permute-start
  282.6 25.9 %collective-permute-done = f32[2,2,256,256]{3,2,1,0:T(8,128)} collective-permute-done((f32[2,2,256,256]{3,2,1,0:T(8,128)}, f32[2,2,256,256]{3,2,1,0:T(8,128)}, u32[]{:S(2)}, u32[]{:S(2)}) %collective-permute-start) | collective-permute-done | bytes 1048608 | tf_op jit(solution)/shard_map/while/body/eval_jaxpr/ppermute | solution.py:10
  319.1 1.9 collective-permute-start
  321.0 26.7 %collective-permute-done = f32[2,2,256,256]{3,2,1,0:T(8,128)} collective-permute-done((f32[2,2,256,256]{3,2,1,0:T(8,128)}, f32[2,2,256,256]{3,2,1,0:T(8,128)}, u32[]{:S(2)}, u32[]{:S(2)}) %collective-permute-start) | collective-permute-done | bytes 1048608 | tf_op jit(solution)/shard_map/while/body/eval_jaxpr/ppermute | solution.py:10
  360.3 25.9 %collective-permute-done = f32[2,2,256,256]{3,2,1,0:T(8,128)} collective-permute-done((f32[2,2,256,256]{3,2,1,0:T(8,128)}, f32[2,2,256,256]{3,2,1,0:T(8,128)}, u32[]{:S(2)}, u32[]{:S(2)}) %collective-permute-start) | collective-permute-done | bytes 1048608 | tf_op jit(solution)/shard_map/while/body/eval_jaxpr/ppermute | solution.py:10
  396.8 1.9 collective-permute-start
  398.7 25.0 %collective-permute-done = f32[2,2,256,256]{3,2,1,0:T(8,128)} collective-permute-done((f32[2,2,256,256]{3,2,1,0:T(8,128)}, f32[2,2,256,256]{3,2,1,0:T(8,128)}, u32[]{:S(2)}, u32[]{:S(2)}) %collective-permute-start) | collective-permute-done | bytes 1048608 | tf_op jit(solution)/shard_map/while/body/eval_jaxpr/ppermute | solution.py:10
  434.4 1.9 collective-permute-start
  436.3 24.2 %collective-permute-done = f32[2,2,256,256]{3,2,1,0:T(8,128)} collective-permute-done((f32[2,2,256,256]{3,2,1,0:T(8,128)}, f32[2,2,256,256]{3,2,1,0:T(8,128)}, u32[]{:S(2)}, u32[]{:S(2)}) %collective-permute-start) | collective-permute-done | bytes 1048608 | tf_op jit(solution)/shard_map/while/body/eval_jaxpr/ppermute | solution.py:10
  471.2 1.9 collective-permute-start
  473.1 23.3 %collective-permute-done = f32[2,2,256,256]{3,2,1,0:T(8,128)} collective-permute-done((f32[2,2,256,256]{3,2,1,0:T(8,128)}, f32[2,2,256,256]{3,2,1,0:T(8,128)}, u32[]{:S(2)}, u32[]{:S(2)}) %collective-permute-start) | collective-permute-done | bytes 1048608 | tf_op jit(solution)/shard_map/while/body/eval_jaxpr/ppermute | solution.py:10
  507.0 1.9 collective-permute-start
  509.0 22.4 %collective-permute-done = f32[2,2,256,256]{3,2,1,0:T(8,128)} collective-permute-done((f32[2,2,256,256]{3,2,1,0:T(8,128)}, f32[2,2,256,256]{3,2,1,0:T(8,128)}, u32[]{:S(2)}, u32[]{:S(2)}) %collective-permute-start) | collective-permute-done | bytes 1048608 | tf_op jit(solution)/shard_map/while/body/eval_jaxpr/ppermute | solution.py:10
  542.1 1.9 collective-permute-start
  544.0 21.6 %collective-permute-done = f32[2,2,256,256]{3,2,1,0:T(8,128)} collective-permute-done((f32[2,2,256,256]{3,2,1,0:T(8,128)}, f32[2,2,256,256]{3,2,1,0:T(8,128)}, u32[]{:S(2)}, u32[]{:S(2)}) %collective-permute-start) | collective-permute-done | bytes 1048608 | tf_op jit(solution)/shard_map/while/body/eval_jaxpr/ppermute | solution.py:10
  578.2 20.7 %collective-permute-done = f32[2,2,256,256]{3,2,1,0:T(8,128)} collective-permute-done((f32[2,2,256,256]{3,2,1,0:T(8,128)}, f32[2,2,256,256]{3,2,1,0:T(8,128)}, u32[]{:S(2)}, u32[]{:S(2)}) %collective-permute-start) | collective-permute-done | bytes 1048608 | tf_op jit(solution)/shard_map/while/body/eval_jaxpr/ppermute | solution.py:10
  609.5 1.9 collective-permute-start
  611.5 19.9 %collective-permute-done = f32[2,2,256,256]{3,2,1,0:T(8,128)} collective-permute-done((f32[2,2,256,256]{3,2,1,0:T(8,128)}, f32[2,2,256,256]{3,2,1,0:T(8,128)}, u32[]{:S(2)}, u32[]{:S(2)}) %collective-permute-start) | collective-permute-done | bytes 1048608 | tf_op jit(solution)/shard_map/while/body/eval_jaxpr/ppermute | solution.py:10
  643.9 19.0 %collective-permute-done = f32[2,2,256,256]{3,2,1,0:T(8,128)} collective-permute-done((f32[2,2,256,256]{3,2,1,0:T(8,128)}, f32[2,2,256,256]{3,2,1,0:T(8,128)}, u32[]{:S(2)}, u32[]{:S(2)}) %collective-permute-start) | collective-permute-done | bytes 1048608 | tf_op jit(solution)/shard_map/while/body/eval_jaxpr/ppermute | solution.py:10
  673.6 1.9 collective-permute-start
  675.5 18.2 %collective-permute-done = f32[2,2,256,256]{3,2,1,0:T(8,128)} collective-permute-done((f32[2,2,256,256]{3,2,1,0:T(8,128)}, f32[2,2,256,256]{3,2,1,0:T(8,128)}, u32[]{:S(2)}, u32[]{:S(2)}) %collective-permute-start) | collective-permute-done | bytes 1048608 | tf_op jit(solution)/shard_map/while/body/eval_jaxpr/ppermute | solution.py:10
  706.2 17.3 %collective-permute-done = f32[2,2,256,256]{3,2,1,0:T(8,128)} collective-permute-done((f32[2,2,256,256]{3,2,1,0:T(8,128)}, f32[2,2,256,256]{3,2,1,0:T(8,128)}, u32[]{:S(2)}, u32[]{:S(2)}) %collective-permute-start) | collective-permute-done | bytes 1048608 | tf_op jit(solution)/shard_map/while/body/eval_jaxpr/ppermute | solution.py:10
  736.1 17.2 %collective-permute-done = f32[2,2,256,256]{3,2,1,0:T(8,128)} collective-permute-done((f32[2,2,256,256]{3,2,1,0:T(8,128)}, f32[2,2,256,256]{3,2,1,0:T(8,128)}, u32[]{:S(2)}, u32[]{:S(2)}) %collective-permute-start) | collective-permute-done | bytes 1048608 | tf_op jit(solution)/shard_map/while/body/eval_jaxpr/ppermute | solution.py:10
  765.9 17.2 %collective-permute-done = f32[2,2,256,256]{3,2,1,0:T(8,128)} collective-permute-done((f32[2,2,256,256]{3,2,1,0:T(8,128)}, f32[2,2,256,256]{3,2,1,0:T(8,128)}, u32[]{:S(2)}, u32[]{:S(2)}) %collective-permute-start) | collective-permute-done | bytes 1048608 | tf_op jit(solution)/shard_map/while/body/eval_jaxpr/ppermute | solution.py:10
  783.2 2.2 fusion.56
  785.5 2.1 fusion.52
  787.6 2.1 convolution_subtract_fusion.10
  790.3 2.2 convolution_add_fusion.10
  816.5 2.4 copy.409
  (337 shorter events, 260.1 us)
Async XLA Ops:
  4.5 28.9 %all-to-all-start = ((bf16[2,2,4,256,256]{4,2,1,0,3:T(4,128)(2,1)}), bf16[2,2,4,256,256]{4,2,1,0,3:T(4,128)(2,1)}, u32[]{:S(2)}, u32[]{:S(2)}) async-start(bf16[2,2,4,256,256]{4,2,1,0,3:T(4,128)(2,1)} %copy.324), calls=%async_computation | async-start | bytes 4194304 | tf_op jit(solution)/shard_map/all_to_all | solution.py:77
  9.3 4.7 copy-start.4
  14.0 1.6 copy-start.17
  14.2 2.5 copy-start.14
  14.2 4.3 copy-start.12
  20.3 21.1 %copy-start.15 = (bf16[1,2,4,256,256]{4,3,2,1,0:T(8,128)(2,1)S(1)}, bf16[1,2,4,256,256]{4,3,2,1,0:T(8,128)(2,1)}, u32[]{:S(2)}) copy-start(bf16[1,2,4,256,256]{4,3,2,1,0:T(8,128)(2,1)} %copy-done.14) | copy-start | bytes 3145732
  33.5 32.0 %all-to-all-start.1 = ((bf16[2,2,4,256,256]{4,2,1,0,3:T(4,128)(2,1)}), bf16[2,2,4,256,256]{4,2,1,0,3:T(4,128)(2,1)}, u32[]{:S(2)}, u32[]{:S(2)}) async-start(bf16[2,2,4,256,256]{4,2,1,0,3:T(4,128)(2,1)} %copy.326), calls=%async_computation.1 | async-start | bytes 4194304 | tf_op jit(solution)/shard_map/all_to_all | solution.py:78
  43.7 4.1 copy-start
  44.7 3.0 copy-start.18
  203.1 31.5 %all-to-all-start.2 = ((bf16[2,16,4,32,256]{4,3,2,0,1:T(8,128)(2,1)}), bf16[2,16,4,32,256]{4,3,2,0,1:T(8,128)(2,1)}, u32[]{:S(2)}, u32[]{:S(2)}) async-start(bf16[2,16,4,32,256]{4,3,2,0,1:T(8,128)(2,1)} %pad_maximum_fusion.2), calls=%async_computation.2 | async-start | bytes 4194304 | tf_op jit(solution)/shard_map/all_to_all | solution.py:80
  212.7 3.6 copy-start.1
  236.6 1.6 copy-start.5
  241.5 1.2 copy-start.16
  243.2 20.8 %copy-start.6 = (f32[2,4,256,256]{3,2,0,1:T(8,128)}, f32[2,4,256,256]{3,2,0,1:T(8,128)S(1)}, u32[]{:S(2)}) copy-start(f32[2,4,256,256]{3,2,0,1:T(8,128)S(1)} %convolution_subtract_fusion.2) | copy-start | bytes 6291460
  244.3 1.8 copy-start.2
  245.0 20.5 %copy-start.8 = (f32[2,4,256,256]{3,2,1,0:T(8,128)}, f32[2,4,256,256]{3,2,1,0:T(8,128)S(1)}, u32[]{:S(2)}) copy-start(f32[2,4,256,256]{3,2,1,0:T(8,128)S(1)} %convolution_add_fusion.2) | copy-start | bytes 6291460
  273.8 2.5 copy-start.10
  275.6 1.4 copy-start.11
  278.7 29.7 %collective-permute-start = (f32[2,2,256,256]{3,2,1,0:T(8,128)}, f32[2,2,256,256]{3,2,1,0:T(8,128)}, u32[]{:S(2)}, u32[]{:S(2)}) collective-permute-start(f32[2,2,256,256]{3,2,1,0:T(8,128)} %pad_maximum_fusion.4), channel_id=1, source_target_pairs={{0,8},{8,16},{16,24},{24,32},{32,40},{40,48},{48,56},{56,64},{64,7... | collective-permute-start | bytes 3145736 | tf_op jit(solution)/shard_map/while/body/eval_jaxpr/ppermute | solution.py:10
  314.2 2.5 copy-start.10
  316.0 1.4 copy-start.11
  319.1 28.7 %collective-permute-start = (f32[2,2,256,256]{3,2,1,0:T(8,128)}, f32[2,2,256,256]{3,2,1,0:T(8,128)}, u32[]{:S(2)}, u32[]{:S(2)}) collective-permute-start(f32[2,2,256,256]{3,2,1,0:T(8,128)} %pad_maximum_fusion.4), channel_id=1, source_target_pairs={{0,8},{8,16},{16,24},{24,32},{32,40},{40,48},{48,56},{56,64},{64,7... | collective-permute-start | bytes 3145736 | tf_op jit(solution)/shard_map/while/body/eval_jaxpr/ppermute | solution.py:10
  353.5 2.5 copy-start.10
  355.3 1.4 copy-start.11
  358.4 27.8 %collective-permute-start = (f32[2,2,256,256]{3,2,1,0:T(8,128)}, f32[2,2,256,256]{3,2,1,0:T(8,128)}, u32[]{:S(2)}, u32[]{:S(2)}) collective-permute-start(f32[2,2,256,256]{3,2,1,0:T(8,128)} %pad_maximum_fusion.4), channel_id=1, source_target_pairs={{0,8},{8,16},{16,24},{24,32},{32,40},{40,48},{48,56},{56,64},{64,7... | collective-permute-start | bytes 3145736 | tf_op jit(solution)/shard_map/while/body/eval_jaxpr/ppermute | solution.py:10
  391.9 2.5 copy-start.10
  393.7 1.4 copy-start.11
  396.8 26.9 %collective-permute-start = (f32[2,2,256,256]{3,2,1,0:T(8,128)}, f32[2,2,256,256]{3,2,1,0:T(8,128)}, u32[]{:S(2)}, u32[]{:S(2)}) collective-permute-start(f32[2,2,256,256]{3,2,1,0:T(8,128)} %pad_maximum_fusion.4), channel_id=1, source_target_pairs={{0,8},{8,16},{16,24},{24,32},{32,40},{40,48},{48,56},{56,64},{64,7... | collective-permute-start | bytes 3145736 | tf_op jit(solution)/shard_map/while/body/eval_jaxpr/ppermute | solution.py:10
  429.5 2.5 copy-start.10
  431.3 1.4 copy-start.11
  434.4 26.1 %collective-permute-start = (f32[2,2,256,256]{3,2,1,0:T(8,128)}, f32[2,2,256,256]{3,2,1,0:T(8,128)}, u32[]{:S(2)}, u32[]{:S(2)}) collective-permute-start(f32[2,2,256,256]{3,2,1,0:T(8,128)} %pad_maximum_fusion.4), channel_id=1, source_target_pairs={{0,8},{8,16},{16,24},{24,32},{32,40},{40,48},{48,56},{56,64},{64,7... | collective-permute-start | bytes 3145736 | tf_op jit(solution)/shard_map/while/body/eval_jaxpr/ppermute | solution.py:10
  466.3 2.5 copy-start.10
  468.1 1.4 copy-start.11
  471.2 25.2 %collective-permute-start = (f32[2,2,256,256]{3,2,1,0:T(8,128)}, f32[2,2,256,256]{3,2,1,0:T(8,128)}, u32[]{:S(2)}, u32[]{:S(2)}) collective-permute-start(f32[2,2,256,256]{3,2,1,0:T(8,128)} %pad_maximum_fusion.4), channel_id=1, source_target_pairs={{0,8},{8,16},{16,24},{24,32},{32,40},{40,48},{48,56},{56,64},{64,7... | collective-permute-start | bytes 3145736 | tf_op jit(solution)/shard_map/while/body/eval_jaxpr/ppermute | solution.py:10
  502.2 2.5 copy-start.10
  503.9 1.4 copy-start.11
  507.0 24.4 %collective-permute-start = (f32[2,2,256,256]{3,2,1,0:T(8,128)}, f32[2,2,256,256]{3,2,1,0:T(8,128)}, u32[]{:S(2)}, u32[]{:S(2)}) collective-permute-start(f32[2,2,256,256]{3,2,1,0:T(8,128)} %pad_maximum_fusion.4), channel_id=1, source_target_pairs={{0,8},{8,16},{16,24},{24,32},{32,40},{40,48},{48,56},{56,64},{64,7... | collective-permute-start | bytes 3145736 | tf_op jit(solution)/shard_map/while/body/eval_jaxpr/ppermute | solution.py:10
  537.2 2.5 copy-start.10
  539.0 1.4 copy-start.11
  542.1 23.5 %collective-permute-start = (f32[2,2,256,256]{3,2,1,0:T(8,128)}, f32[2,2,256,256]{3,2,1,0:T(8,128)}, u32[]{:S(2)}, u32[]{:S(2)}) collective-permute-start(f32[2,2,256,256]{3,2,1,0:T(8,128)} %pad_maximum_fusion.4), channel_id=1, source_target_pairs={{0,8},{8,16},{16,24},{24,32},{32,40},{40,48},{48,56},{56,64},{64,7... | collective-permute-start | bytes 3145736 | tf_op jit(solution)/shard_map/while/body/eval_jaxpr/ppermute | solution.py:10
  571.4 2.5 copy-start.10
  573.1 1.4 copy-start.11
  576.2 22.7 %collective-permute-start = (f32[2,2,256,256]{3,2,1,0:T(8,128)}, f32[2,2,256,256]{3,2,1,0:T(8,128)}, u32[]{:S(2)}, u32[]{:S(2)}) collective-permute-start(f32[2,2,256,256]{3,2,1,0:T(8,128)} %pad_maximum_fusion.4), channel_id=1, source_target_pairs={{0,8},{8,16},{16,24},{24,32},{32,40},{40,48},{48,56},{56,64},{64,7... | collective-permute-start | bytes 3145736 | tf_op jit(solution)/shard_map/while/body/eval_jaxpr/ppermute | solution.py:10
  604.7 2.5 copy-start.10
  606.4 1.4 copy-start.11
  609.5 21.8 %collective-permute-start = (f32[2,2,256,256]{3,2,1,0:T(8,128)}, f32[2,2,256,256]{3,2,1,0:T(8,128)}, u32[]{:S(2)}, u32[]{:S(2)}) collective-permute-start(f32[2,2,256,256]{3,2,1,0:T(8,128)} %pad_maximum_fusion.4), channel_id=1, source_target_pairs={{0,8},{8,16},{16,24},{24,32},{32,40},{40,48},{48,56},{56,64},{64,7... | collective-permute-start | bytes 3145736 | tf_op jit(solution)/shard_map/while/body/eval_jaxpr/ppermute | solution.py:10
  637.1 2.5 copy-start.10
  638.9 1.4 copy-start.11
  642.0 20.9 %collective-permute-start = (f32[2,2,256,256]{3,2,1,0:T(8,128)}, f32[2,2,256,256]{3,2,1,0:T(8,128)}, u32[]{:S(2)}, u32[]{:S(2)}) collective-permute-start(f32[2,2,256,256]{3,2,1,0:T(8,128)} %pad_maximum_fusion.4), channel_id=1, source_target_pairs={{0,8},{8,16},{16,24},{24,32},{32,40},{40,48},{48,56},{56,64},{64,7... | collective-permute-start | bytes 3145736 | tf_op jit(solution)/shard_map/while/body/eval_jaxpr/ppermute | solution.py:10
  668.7 2.5 copy-start.10
  670.5 1.4 copy-start.11
  673.6 20.1 %collective-permute-start = (f32[2,2,256,256]{3,2,1,0:T(8,128)}, f32[2,2,256,256]{3,2,1,0:T(8,128)}, u32[]{:S(2)}, u32[]{:S(2)}) collective-permute-start(f32[2,2,256,256]{3,2,1,0:T(8,128)} %pad_maximum_fusion.4), channel_id=1, source_target_pairs={{0,8},{8,16},{16,24},{24,32},{32,40},{40,48},{48,56},{56,64},{64,7... | collective-permute-start | bytes 3145736 | tf_op jit(solution)/shard_map/while/body/eval_jaxpr/ppermute | solution.py:10
  699.4 2.5 copy-start.10
  701.2 1.4 copy-start.11
  704.3 19.2 %collective-permute-start = (f32[2,2,256,256]{3,2,1,0:T(8,128)}, f32[2,2,256,256]{3,2,1,0:T(8,128)}, u32[]{:S(2)}, u32[]{:S(2)}) collective-permute-start(f32[2,2,256,256]{3,2,1,0:T(8,128)} %pad_maximum_fusion.4), channel_id=1, source_target_pairs={{0,8},{8,16},{16,24},{24,32},{32,40},{40,48},{48,56},{56,64},{64,7... | collective-permute-start | bytes 3145736 | tf_op jit(solution)/shard_map/while/body/eval_jaxpr/ppermute | solution.py:10
  729.3 2.5 copy-start.10
  731.1 1.4 copy-start.11
  734.2 19.1 %collective-permute-start = (f32[2,2,256,256]{3,2,1,0:T(8,128)}, f32[2,2,256,256]{3,2,1,0:T(8,128)}, u32[]{:S(2)}, u32[]{:S(2)}) collective-permute-start(f32[2,2,256,256]{3,2,1,0:T(8,128)} %pad_maximum_fusion.4), channel_id=1, source_target_pairs={{0,8},{8,16},{16,24},{24,32},{32,40},{40,48},{48,56},{56,64},{64,7... | collective-permute-start | bytes 3145736 | tf_op jit(solution)/shard_map/while/body/eval_jaxpr/ppermute | solution.py:10
  759.1 2.5 copy-start.10
  760.8 1.4 copy-start.11
  763.9 19.1 %collective-permute-start = (f32[2,2,256,256]{3,2,1,0:T(8,128)}, f32[2,2,256,256]{3,2,1,0:T(8,128)}, u32[]{:S(2)}, u32[]{:S(2)}) collective-permute-start(f32[2,2,256,256]{3,2,1,0:T(8,128)} %pad_maximum_fusion.4), channel_id=1, source_target_pairs={{0,8},{8,16},{16,24},{24,32},{32,40},{40,48},{48,56},{56,64},{64,7... | collective-permute-start | bytes 3145736 | tf_op jit(solution)/shard_map/while/body/eval_jaxpr/ppermute | solution.py:10
  783.2 4.4 copy-start.3
  790.3 2.9 copy-start.9
  792.6 1.6 copy-start.7
  (1 other events, 1.2 us)
where the time goes:
time: 828 us; the launch traced here: 819 us
  waiting for transfers between devices  359 us (43%)
  matrix products  224 us (27%)
  other arithmetic  140 us (17%)
  starting transfers between devices  50.8 us (6%)
  local copies, waits for them, and re-layouts  42.3 us (5%)
    ppermute x15, waiting for transfers between devices, from_behind(): return lax.ppermute(x, axis, pairs)  324 us
    dot_general x100, matrix products, precise(): jnp.einsum('eij,ejk->eik', first, second, precision=lax.Precision.HIGHEST...  154 us
    add x16, other arithmetic, add_offset(): imag_part = totals[1] + shifted[0] * weight[1] + shifted[1] * weight[0]  110 us
    dot_general x88, matrix products, precise_adjoint(): jnp.einsum('eij,ekj->eik', first, second, precision=lax.Precision.HIGHEST...  60.3 us
    ppermute x15, starting transfers between devices, from_behind(): return lax.ppermute(x, axis, pairs)  30.6 us
  transfers between devices with their start and end apart: 18, of which 18 were waited for; matrix products, arithmetic and copies ran while one was open for 4% of the time, Pallas kernels for 0%

commit v1 on v0

v1 whole, which is shorter than its diff:
```python
import jax
import jax.numpy as jnp
from jax import lax
from jax.experimental import pallas as pl
from jax.experimental.pallas import tpu as pltpu
from jax.sharding import PartitionSpec as P

F32 = jnp.float32
BF16 = jnp.bfloat16
NORB = 256
POINTS = 16
MIDDLE = POINTS // 2
PEERS = 8
STRIPE = NORB // PEERS
SLABS = 4
EN = 2
SIDE = 4
MESH = pl.DeviceIdType.MESH


def nn(a, b):
    return lax.dot_general(a, b, (((1,), (0,)), ((), ())), preferred_element_type=F32)


def nt(a, b):
    return lax.dot_general(a, b, (((1,), (1,)), ((), ())), preferred_element_type=F32)


def rows(pair):
    return pair.reshape(2 * NORB, NORB)


def left(x3, re, im):
    return nn(rows(x3[1:3]), re) + nn(rows(x3[0:2]), im)


def right(i3, x3):
    return nt(rows(i3[1:3]), x3[1]) + nt(rows(i3[0:2]), x3[0])


def split(value):
    high = value.astype(BF16)
    low = (value - high.astype(F32)).astype(BF16)
    return high, low


def put3(ref, pair):
    ref[1:3] = pair.reshape(2, NORB, NORB)
    ref[0] = -pair[NORB:]


def product(xh, xl, ch, cl):
    total = left(xh, ch[:NORB], ch[NORB:]) + left(xh, cl[:NORB], cl[NORB:])
    if xl is not None:
        total = total + left(xl, ch[:NORB], ch[NORB:])
    return total


def congruence(xh, xl, state, ih, il):
    high, low = split(state)
    inner = product(xh, xl, high, low)
    high, low = split(inner)
    put3(ih, high)
    put3(il, low)
    total = right(ih, xh) + right(il, xh)
    if xl is not None:
        total = total + right(ih, xl)
    return total


def kernel(
    g_hbm, w_hbm, r_hbm, t_hbm, out_hbm,
    gbuf, wbuf, sig, smat, g3, coup, kh, kl, ph, pw, qh, ql, bst,
    mh, ml, nh, nl, arow, rrow, zh, zl, pre, ih, il, gf, wf,
    fs, fr, rs, rr, ms, mr, ns, nr, asend, arecv, xs, xr, ld, od,
):
    slab = lax.axis_index("slab")
    me = lax.axis_index("energy")
    x = slab // SIDE
    z = slab % SIDE

    def energy_peer(k):
        return {"energy": (me + k) % PEERS}

    def z_peer(k):
        return {"slab": x * SIDE + (z + k) % SIDE}

    def x_peer(k):
        return {"slab": ((x + k) % SIDE) * SIDE + z}

    barrier = pltpu.get_barrier_semaphore()
    for k in range(1, PEERS):
        pl.semaphore_signal(barrier, inc=1, device_id=energy_peer(k), device_id_type=MESH)
    for k in range(1, SIDE):
        pl.semaphore_signal(barrier, inc=1, device_id=z_peer(k), device_id_type=MESH)
        pl.semaphore_signal(barrier, inc=1, device_id=x_peer(k), device_id_type=MESH)

    loads = []
    for e in range(EN):
        for s in range(SLABS):
            cp = pltpu.make_async_copy(r_hbm.at[:, e, s], g3.at[e, s, pl.ds(1, 2)], ld.at[e, s])
            cp.start()
            loads.append(cp)
    cp = pltpu.make_async_copy(t_hbm, coup, ld.at[0, SLABS])
    cp.start()
    loads.append(cp)

    def stripe(p):
        return pl.ds(pl.multiple_of(p * STRIPE, STRIPE), STRIPE)

    own = pl.ds(2 * me, EN)
    arrays = ((g_hbm, gbuf), (w_hbm, wbuf))

    def local_stripe(a, s):
        return pltpu.make_async_copy(
            arrays[a][0].at[:, :, s, stripe(me)], arrays[a][1].at[s, :, own], fr.at[a, s, 0]
        )

    def forward(a, s, k):
        p = (me + k) % PEERS
        return pltpu.make_async_remote_copy(
            src_ref=arrays[a][0].at[:, :, s, stripe(p)],
            dst_ref=arrays[a][1].at[s, :, own],
            send_sem=fs.at[a, s, k],
            recv_sem=fr.at[a, s, k],
            device_id={"energy": p},
            device_id_type=MESH,
        )

    pl.semaphore_wait(barrier, PEERS - 1 + 2 * (SIDE - 1))
    for s in range(SLABS):
        for k in range(1, PEERS):
            for a in range(2):
                forward(a, s, k).start()
        for a in range(2):
            local_stripe(a, s).start()

    def gather(k, source, target, send, recv, peer):
        return pltpu.make_async_remote_copy(
            src_ref=source, dst_ref=target, send_sem=send, recv_sem=recv,
            device_id=peer, device_id_type=MESH,
        )

    def send_m(e, k, i):
        view = (mh, ml)[i].at[z, e, pl.ds(1, 2)]
        return gather(k, view, view, ms.at[i, e, k], mr.at[i, e, k], z_peer(k))

    def send_n(e, k, i):
        view = (nh, nl)[i].at[x, e, pl.ds(1, 2)]
        return gather(k, view, view, ns.at[i, e, k], nr.at[i, e, k], x_peer(k))

    def upward(act):
        for k in range(1, SIDE):
            pl.when(x + k < SIDE)(lambda k=k: act(k))

    def from_below(act):
        for k in range(1, SIDE):
            pl.when(x - k >= 0)(lambda k=k: act(k))

    def send_a(e, k):
        view = arow.at[z, e]
        return gather(k, view, view, asend.at[e, k], arecv.at[e, k], z_peer(k))

    def send_r(e, k):
        view = rrow.at[x, e]
        return gather(k, view, view, xs.at[e, k], xr.at[e, k], x_peer(k))

    for cp in loads:
        cp.wait()

    @pl.loop(0, EN)
    def _(e):
        @pl.loop(0, SLABS)
        def _(s):
            g3[e, s, 0] = -g3[e, s, 2]
            high, low = split(left(g3[e, s], coup[0, s], coup[1, s]))
            put3(kh.at[e, s], high)
            put3(kl.at[e, s], low)

        ph[e, 0] = kh[e, 0]
        pw[e, 0] = kl[e, 0]

        @pl.loop(1, SLABS)
        def _(s):
            value = product(kh[e, s], kl[e, s], rows(ph[e, s - 1, 1:3]), rows(pw[e, s - 1, 1:3]))
            high, low = split(value)
            put3(ph.at[e, s], high)
            put3(pw.at[e, s], low)

        mh[z, e] = ph[e, SLABS - 1]
        ml[z, e] = pw[e, SLABS - 1]
        for i in range(2):
            for k in range(1, SIDE):
                send_m(e, k, i).start()

    def convolve(s):
        for a in range(2):
            local_stripe(a, s).wait()
        for k in range(1, PEERS):
            for a in range(2):
                forward(a, s, k).wait_recv()

        @pl.loop(0, STRIPE // 16)
        def _(tr):
            @pl.loop(0, NORB // 128)
            def _(tc):
                rr_ = pl.ds(pl.multiple_of(tr * 16, 16), 16)
                cc_ = pl.ds(pl.multiple_of(tc * 128, 128), 128)
                for part in range(2):
                    for m in range(POINTS):
                        gf[part, m] = gbuf[s, part, m, rr_, cc_].astype(F32)
                        wf[part, m] = wbuf[s, part, m, rr_, cc_].astype(F32)
                for n in range(POINTS):
                    re = None
                    im = None
                    for m in range(max(0, n + MIDDLE + 1 - POINTS), min(POINTS, n + MIDDLE + 1)):
                        l = n - m + MIDDLE
                        a, b = gf[0, m], gf[1, m]
                        c, d = wf[0, l], wf[1, l]
                        r = a * c - b * d
                        i = a * d + b * c
                        re = r if re is None else re + r
                        im = i if im is None else im + i
                    sig[s, 0, n, rr_, cc_] = (im * (-1.0 / POINTS)).astype(BF16)
                    sig[s, 1, n, rr_, cc_] = (re * (1.0 / POINTS)).astype(BF16)

    parts = (pl.ds(0, SLABS - 1), pl.ds(SLABS - 1, 1))

    def giveback(e, part, k):
        p = (me + k) % PEERS
        return pltpu.make_async_remote_copy(
            src_ref=sig.at[parts[part], :, 2 * p + e],
            dst_ref=smat.at[e, parts[part], :, stripe(me)],
            send_sem=rs.at[e, part, k],
            recv_sem=rr.at[e, part, k],
            device_id={"energy": p},
            device_id_type=MESH,
        )

    def keep(e, part):
        return pltpu.make_async_copy(
            sig.at[parts[part], :, 2 * me + e], smat.at[e, parts[part], :, stripe(me)], rr.at[e, part, 0]
        )

    def row_products(e):
        for i in range(2):
            for k in range(1, SIDE):
                send_m(e, k, i).wait_recv()
        eye = (
            lax.broadcasted_iota(jnp.int32, (NORB, NORB), 0)
            == lax.broadcasted_iota(jnp.int32, (NORB, NORB), 1)
        )
        zh[0, 0] = jnp.zeros((NORB, NORB), BF16)
        zh[0, 1] = jnp.where(eye, 1.0, 0.0).astype(BF16)
        zh[0, 2] = jnp.zeros((NORB, NORB), BF16)
        zl[0] = jnp.zeros((3, NORB, NORB), BF16)

        @pl.loop(0, SIDE)
        def _(j):
            mh[j, e, 0] = -mh[j, e, 2]
            ml[j, e, 0] = -ml[j, e, 2]
            value = product(mh[j, e], ml[j, e], rows(zh[j, 1:3]), rows(zl[j, 1:3]))
            high, low = split(value)
            put3(zh.at[j + 1], high)
            put3(zl.at[j + 1], low)

        nh[x, e] = zh[SIDE]
        nl[x, e] = zl[SIDE]

        @pl.when(x > 0)
        def _():
            for i in range(2):
                upward(lambda k: send_n(e, k, i).start())

        @pl.loop(0, SLABS)
        def _(s):
            value = product(ph[e, s], pw[e, s], rows(zh[z, 1:3]), rows(zl[z, 1:3]))
            high, low = split(value)
            put3(qh.at[e, s], high)
            put3(ql.at[e, s], low)

    @pl.loop(0, SLABS - 2)
    def _(s):
        convolve(s)

    row_products(0)
    convolve(SLABS - 2)
    for k in range(1, PEERS):
        giveback(0, 0, k).start()
    keep(0, 0).start()
    convolve(SLABS - 1)
    for e, part in ((0, 1), (1, 0), (1, 1)):
        for k in range(1, PEERS):
            giveback(e, part, k).start()
        keep(e, part).start()
    row_products(1)

    @pl.loop(0, EN)
    def _(e):
        for part in range(2):
            keep(e, part).wait()
            for k in range(1, PEERS):
                giveback(e, part, k).wait_recv()

        @pl.loop(0, SLABS)
        def _(s):
            mixed = left(g3[e, s], smat[e, s, 0], smat[e, s, 1]).astype(BF16)
            put3(ih, mixed)
            bst[e, s] = right(ih, g3[e, s]).reshape(2, NORB, NORB)

        @pl.loop(1, SLABS)
        def _(s):
            value = congruence(kh[e, s], kl[e, s], rows(bst[e, s - 1]), ih, il)
            bst[e, s] += value.reshape(2, NORB, NORB)

        arow[z, e] = bst[e, SLABS - 1].astype(BF16)
        for k in range(1, SIDE):
            send_a(e, k).start()

    def scan(e, high, low, values, count):
        pre[0] = jnp.zeros((2, NORB, NORB), F32)
        pre[1] = values[0, e].astype(F32)

        @pl.loop(1, count)
        def _(j):
            value = congruence(high[j, e], low[j, e], rows(pre[j]), ih, il)
            pre[j + 1] = value.reshape(2, NORB, NORB) + values[j, e].astype(F32)

    def spread(e, high, low, index):
        @pl.loop(0, SLABS)
        def _(s):
            value = congruence(high[e, s], low[e, s], rows(pre[index]), ih, il)
            bst[e, s] += value.reshape(2, NORB, NORB)

    @pl.loop(0, EN)
    def _(e):
        for k in range(1, SIDE):
            send_a(e, k).wait_recv()
        scan(e, mh, ml, arow, SIDE)
        rrow[x, e] = pre[SIDE].astype(BF16)
        upward(lambda k: send_r(e, k).start())
        spread(e, ph, pw, z)

    def store(e, s):
        return pltpu.make_async_copy(bst.at[e, s], out_hbm.at[:, e, s], od.at[e, s])

    @pl.loop(0, EN)
    def _(e):
        from_below(lambda k: send_r(e, k).wait_recv())

        @pl.when(x > 0)
        def _():
            for k in range(1, SIDE - 1):

                @pl.when(x - k > 0)
                def _(k=k):
                    for i in range(2):
                        send_n(e, k, i).wait_recv()

            pre[1] = rrow[0, e].astype(F32)

            @pl.loop(1, x)
            def _(j):
                nh[j, e, 0] = -nh[j, e, 2]
                nl[j, e, 0] = -nl[j, e, 2]
                value = congruence(nh[j, e], nl[j, e], rows(pre[j]), ih, il)
                pre[j + 1] = value.reshape(2, NORB, NORB) + rrow[j, e].astype(F32)

            spread(e, qh, ql, x)

        for s in range(SLABS):
            store(e, s).start()

    for e in range(EN):
        for s in range(SLABS):
            store(e, s).wait()
        for k in range(1, SIDE):
            send_m(e, k, 0).wait_send()
            send_m(e, k, 1).wait_send()
            send_a(e, k).wait_send()
        upward(lambda k: send_r(e, k).wait_send())

        @pl.when(x > 0)
        def _(e=e):
            for i in range(2):
                upward(lambda k: send_n(e, k, i).wait_send())

        for part in range(2):
            for k in range(1, PEERS):
                giveback(e, part, k).wait_send()
    for s in range(SLABS):
        for k in range(1, PEERS):
            for a in range(2):
                forward(a, s, k).wait_send()


def per_device(green_lesser, screened_lesser, green_retarded, coupling):
    block = (NORB, NORB)
    dma = pltpu.SemaphoreType.DMA
    return pl.pallas_call(
        kernel,
        out_shape=jax.ShapeDtypeStruct((2, EN, SLABS) + block, F32),
        in_specs=[pl.BlockSpec(memory_space=pl.ANY)] * 4,
        out_specs=pl.BlockSpec(memory_space=pl.ANY),
        scratch_shapes=[
            pltpu.VMEM((SLABS, 2, POINTS, STRIPE, NORB), BF16),
            pltpu.VMEM((SLABS, 2, POINTS, STRIPE, NORB), BF16),
            pltpu.VMEM((SLABS, 2, POINTS, STRIPE, NORB), BF16),
            pltpu.VMEM((EN, SLABS, 2) + block, BF16),
            pltpu.VMEM((EN, SLABS, 3) + block, BF16),
            pltpu.VMEM((2, SLABS) + block, BF16),
            pltpu.VMEM((EN, SLABS, 3) + block, BF16),
            pltpu.VMEM((EN, SLABS, 3) + block, BF16),
            pltpu.VMEM((EN, SLABS, 3) + block, BF16),
            pltpu.VMEM((EN, SLABS, 3) + block, BF16),
            pltpu.VMEM((EN, SLABS, 3) + block, BF16),
            pltpu.VMEM((EN, SLABS, 3) + block, BF16),
            pltpu.VMEM((EN, SLABS, 2) + block, F32),
            pltpu.VMEM((SIDE, EN, 3) + block, BF16),
            pltpu.VMEM((SIDE, EN, 3) + block, BF16),
            pltpu.VMEM((SIDE, EN, 3) + block, BF16),
            pltpu.VMEM((SIDE, EN, 3) + block, BF16),
            pltpu.VMEM((SIDE, EN, 2) + block, BF16),
            pltpu.VMEM((SIDE, EN, 2) + block, BF16),
            pltpu.VMEM((SIDE + 1, 3) + block, BF16),
            pltpu.VMEM((SIDE + 1, 3) + block, BF16),
            pltpu.VMEM((SIDE + 1, 2) + block, F32),
            pltpu.VMEM((3,) + block, BF16),
            pltpu.VMEM((3,) + block, BF16),
            pltpu.VMEM((2, POINTS, 16, 128), F32),
            pltpu.VMEM((2, POINTS, 16, 128), F32),
            dma((2, SLABS, PEERS)),
            dma((2, SLABS, PEERS)),
            dma((EN, 2, PEERS)),
            dma((EN, 2, PEERS)),
            dma((2, EN, SIDE)),
            dma((2, EN, SIDE)),
            dma((2, EN, SIDE)),
            dma((2, EN, SIDE)),
            dma((EN, SIDE)),
            dma((EN, SIDE)),
            dma((EN, SIDE)),
            dma((EN, SIDE)),
            dma((EN, SLABS + 1)),
            dma((EN, SLABS)),
        ],
        compiler_params=pltpu.CompilerParams(
            collective_id=0, has_side_effects=True, vmem_limit_bytes=63000 * 1024
        ),
        name="born_step",
    )(green_lesser, screened_lesser, green_retarded, coupling)


def solution(mesh):
    placed = (
        P(None, "energy", "slab", None, None),
        P(None, "energy", "slab", None, None),
        P(None, "energy", "slab", None, None),
        P(None, "slab", None, None),
    )
    return jax.shard_map(
        per_device,
        mesh=mesh,
        in_specs=placed,
        out_specs=P(None, "energy", "slab", None, None),
        check_vma=False,
    )
```

time: 828 us -> 144 us (0.17)
  the two profiles are of different devices: /device:TPU:22 before, /device:TPU:31 now
where the time goes in v1:
time: 144 us; the launch traced here: 142 us
  Pallas kernels  138 us (96%)
  local copies, waits for them, and re-layouts  4.6 us (3%)
    pallas_call x1, Pallas kernels, per_device(): pl.pallas_call(kernel, out_shape=jax.ShapeDtypeStruct((2, EN, SLABS) + bl...  138 us
    unnamed x1, local copies, waits for them, and re-layouts  4.6 us

profile of v1, /device:TPU:31, one launch (start us, length us, event | category | flops | bytes accessed | tf_op | source)
XLA Modules:
  0.0 142.1 jit_solution(2520198789621194837)
XLA Ops:
  0.0 137.5 %born_step.1 = f32[2,2,4,256,256]{4,3,2,1,0:T(8,128)} custom-call(bf16[2,2,4,256,256]{4,3,2,1,0:T(8,128)(2,1)} %g_hbm.1, bf16[2,2,4,256,256]{4,3,2,1,0:T(8,128)(2,1)} %w_hbm.1, bf16[2,2,4,256,256]{4,3,2,1,0:T(8,128)(2,1)} %r_hbm.1, bf16[2,4,256,256]{3,2,1,0:T(8,128)(2,1)} %t_hbm.1), custom_call_target="tpu_custom_call" | custom-call | tf_op jit(solution)/shard_map/born_step/pallas_call | solution.py:400
  137.5 4.6 %copy.6 = f32[2,2,4,256,256]{4,3,2,1,0:T(8,128)} copy(f32[2,2,4,256,256]{4,3,2,1,0:T(8,128)} %born_step.1) | data formatting | bytes 8388608

commit v2 on v1

--- a/solution.py
+++ b/solution.py
@@ -50,27 +50,24 @@
 
 
 def product(xh, xl, ch, cl):
-    total = left(xh, ch[:NORB], ch[NORB:]) + left(xh, cl[:NORB], cl[NORB:])
-    if xl is not None:
-        total = total + left(xl, ch[:NORB], ch[NORB:])
+    total = left(xh, ch[:NORB], ch[NORB:]) + left(xl, ch[:NORB], ch[NORB:])
+    if cl is not None:
+        total = total + left(xh, cl[:NORB], cl[NORB:])
     return total
 
 
-def congruence(xh, xl, state, ih, il):
+def congruence(xh, xl, state, ih, il, exact=False):
     high, low = split(state)
-    inner = product(xh, xl, high, low)
+    inner = product(xh, xl, high, None if exact else low)
     high, low = split(inner)
     put3(ih, high)
     put3(il, low)
-    total = right(ih, xh) + right(il, xh)
-    if xl is not None:
-        total = total + right(ih, xl)
-    return total
+    return right(ih, xh) + right(il, xh) + right(ih, xl)
 
 
 def kernel(
     g_hbm, w_hbm, r_hbm, t_hbm, out_hbm,
-    gbuf, wbuf, sig, smat, g3, coup, kh, kl, ph, pw, qh, ql, bst,
+    gbuf, wbuf, sig, smat, g3, coup, kh, kl, ph, pw, yh, yl, bst, cin,
     mh, ml, nh, nl, arow, rrow, zh, zl, pre, ih, il, gf, wf,
     fs, fr, rs, rr, ms, mr, ns, nr, asend, arecv, xs, xr, ld, od,
 ):
@@ -152,10 +149,6 @@
     def upward(act):
         for k in range(1, SIDE):
             pl.when(x + k < SIDE)(lambda k=k: act(k))
-
-    def from_below(act):
-        for k in range(1, SIDE):
-            pl.when(x - k >= 0)(lambda k=k: act(k))
 
     def send_a(e, k):
         view = arow.at[z, e]
@@ -272,12 +265,8 @@
             for i in range(2):
                 upward(lambda k: send_n(e, k, i).start())
 
-        @pl.loop(0, SLABS)
-        def _(s):
-            value = product(ph[e, s], pw[e, s], rows(zh[z, 1:3]), rows(zl[z, 1:3]))
-            high, low = split(value)
-            put3(qh.at[e, s], high)
-            put3(ql.at[e, s], low)
+        yh[e] = zh[z]
+        yl[e] = zl[z]
 
     @pl.loop(0, SLABS - 2)
     def _(s):
@@ -295,80 +284,116 @@
         keep(e, part).start()
     row_products(1)
 
+    def returned(e, part):
+        keep(e, part).wait()
+        for k in range(1, PEERS):
+            giveback(e, part, k).wait_recv()
+
     @pl.loop(0, EN)
     def _(e):
-        for part in range(2):
-            keep(e, part).wait()
-            for k in range(1, PEERS):
-                giveback(e, part, k).wait_recv()
+        returned(e, 0)
 
         @pl.loop(0, SLABS)
         def _(s):
+            @pl.when(s == SLABS - 1)
+            def _():
+                returned(e, 1)
+
             mixed = left(g3[e, s], smat[e, s, 0], smat[e, s, 1]).astype(BF16)
             put3(ih, mixed)
             bst[e, s] = right(ih, g3[e, s]).reshape(2, NORB, NORB)
 
-        @pl.loop(1, SLABS)
-        def _(s):
-            value = congruence(kh[e, s], kl[e, s], rows(bst[e, s - 1]), ih, il)
-            bst[e, s] += value.reshape(2, NORB, NORB)
+            @pl.when(s > 0)
+            def _():
+                value = congruence(kh[e, s], kl[e, s], rows(bst[e, s - 1]), ih, il)
+                bst[e, s] += value.reshape(2, NORB, NORB)
 
         arow[z, e] = bst[e, SLABS - 1].astype(BF16)
-        for k in range(1, SIDE):
+        for k in (2, 1, 3):
             send_a(e, k).start()
 
-    def scan(e, high, low, values, count):
+    top = jnp.where(x < SIDE - 1, SIDE, jnp.maximum(z, 1))
+
+    @pl.loop(0, EN)
+    def _(e):
+        def arrived(j):
+            k = (z - j + SIDE) % SIDE
+
+            @pl.when(k > 0)
+            def _():
+                send_a(e, k).wait_recv()
+
+        def step(j, exact):
+            value = congruence(mh[j, e], ml[j, e], rows(pre[j]), ih, il, exact)
+            pre[j + 1] = value.reshape(2, NORB, NORB)
+            arrived(j)
+            pre[j + 1] += arow[j, e].astype(F32)
+
         pre[0] = jnp.zeros((2, NORB, NORB), F32)
-        pre[1] = values[0, e].astype(F32)
-
-        @pl.loop(1, count)
+        arrived(0)
+        pre[1] = arow[0, e].astype(F32)
+
+        @pl.when(top > 1)
+        def _():
+            step(1, True)
+
+            @pl.loop(2, top)
+            def _(j):
+                step(j, False)
+
+        @pl.loop(top, SIDE)
         def _(j):
-            value = congruence(high[j, e], low[j, e], rows(pre[j]), ih, il)
-            pre[j + 1] = value.reshape(2, NORB, NORB) + values[j, e].astype(F32)
-
-    def spread(e, high, low, index):
+            arrived(j)
+
+        @pl.when(x < SIDE - 1)
+        def _():
+            rrow[x, e] = pre[SIDE].astype(BF16)
+            for k in range(SIDE - 1, 0, -1):
+
+                @pl.when(x + k < SIDE)
+                def _(k=k):
+                    send_r(e, k).start()
+
+        cin[e] = pre[z]
+
+    def store(e, s):
+        return pltpu.make_async_copy(bst.at[e, s], out_hbm.at[:, e, s], od.at[e, s])
+
+    @pl.loop(0, EN)
+    def _(e):
+        def step(j, exact):
+            for i in range(2):
+                send_n(e, x - j, i).wait_recv()
+            nh[j, e, 0] = -nh[j, e, 2]
+            nl[j, e, 0] = -nl[j, e, 2]
+            value = congruence(nh[j, e], nl[j, e], rows(pre[j]), ih, il, exact)
+            pre[j + 1] = value.reshape(2, NORB, NORB)
+            send_r(e, x - j).wait_recv()
+            pre[j + 1] += rrow[j, e].astype(F32)
+
+        @pl.when(x > 0)
+        def _():
+            send_r(e, x).wait_recv()
+            pre[1] = rrow[0, e].astype(F32)
+
+            @pl.when(x > 1)
+            def _():
+                step(1, True)
+
+                @pl.loop(2, x)
+                def _(j):
+                    step(j, False)
+
+            value = congruence(yh[e], yl[e], rows(pre[x]), ih, il)
+            cin[e] += value.reshape(2, NORB, NORB)
+
         @pl.loop(0, SLABS)
         def _(s):
-            value = congruence(high[e, s], low[e, s], rows(pre[index]), ih, il)
-            bst[e, s] += value.reshape(2, NORB, NORB)
-
-    @pl.loop(0, EN)
-    def _(e):
-        for k in range(1, SIDE):
-            send_a(e, k).wait_recv()
-        scan(e, mh, ml, arow, SIDE)
-        rrow[x, e] = pre[SIDE].astype(BF16)
-        upward(lambda k: send_r(e, k).start())
-        spread(e, ph, pw, z)
-
-    def store(e, s):
-        return pltpu.make_async_copy(bst.at[e, s], out_hbm.at[:, e, s], od.at[e, s])
-
-    @pl.loop(0, EN)
-    def _(e):
-        from_below(lambda k: send_r(e, k).wait_recv())
-
-        @pl.when(x > 0)
-        def _():
-            for k in range(1, SIDE - 1):
-
-                @pl.when(x - k > 0)
-                def _(k=k):
-                    for i in range(2):
-                        send_n(e, k, i).wait_recv()
-
-            pre[1] = rrow[0, e].astype(F32)
-
-            @pl.loop(1, x)
-            def _(j):
-                nh[j, e, 0] = -nh[j, e, 2]
-                nl[j, e, 0] = -nl[j, e, 2]
-                value = congruence(nh[j, e], nl[j, e], rows(pre[j]), ih, il)
-                pre[j + 1] = value.reshape(2, NORB, NORB) + rrow[j, e].astype(F32)
-
-            spread(e, qh, ql, x)
-
-        for s in range(SLABS):
+            @pl.when(slab > 0)
+            def _():
+                value = congruence(ph[e, s], pw[e, s], rows(cin[e]), ih, il)
+                bst[e, s] += value.reshape(2, NORB, NORB)
+
             store(e, s).start()
 
     for e in range(EN):
@@ -413,9 +438,10 @@
             pltpu.VMEM((EN, SLABS, 3) + block, BF16),
             pltpu.VMEM((EN, SLABS, 3) + block, BF16),
             pltpu.VMEM((EN, SLABS, 3) + block, BF16),
-            pltpu.VMEM((EN, SLABS, 3) + block, BF16),
-            pltpu.VMEM((EN, SLABS, 3) + block, BF16),
+            pltpu.VMEM((EN, 3) + block, BF16),
+            pltpu.VMEM((EN, 3) + block, BF16),
             pltpu.VMEM((EN, SLABS, 2) + block, F32),
+            pltpu.VMEM((EN, 2) + block, F32),
             pltpu.VMEM((SIDE, EN, 3) + block, BF16),
             pltpu.VMEM((SIDE, EN, 3) + block, BF16),
             pltpu.VMEM((SIDE, EN, 3) + block, BF16),

time: 144 us -> 137 us (0.951)
  Pallas kernels: 138 us -> 131 us
    pallas_call x1, Pallas kernels: 138 us -> 131 us  [per_device(): pl.pallas_call(kernel, out_shape=jax.ShapeDtypeStruct((2, EN, SLABS) + bl...]
where the time goes in v2:
time: 137 us; the launch traced here: 135 us
  Pallas kernels  131 us (96%)
  local copies, waits for them, and re-layouts  4.6 us (3%)
    pallas_call x1, Pallas kernels, per_device(): pl.pallas_call(kernel, out_shape=jax.ShapeDtypeStruct((2, EN, SLABS) + bl...  131 us
    unnamed x1, local copies, waits for them, and re-layouts  4.6 us

profile of v2, /device:TPU:31, one launch (start us, length us, event | category | flops | bytes accessed | tf_op | source)
XLA Modules:
  0.0 135.2 jit_solution(13827891887403421235)
XLA Ops:
  0.0 130.5 %born_step.1 = f32[2,2,4,256,256]{4,3,2,1,0:T(8,128)} custom-call(bf16[2,2,4,256,256]{4,3,2,1,0:T(8,128)(2,1)} %g_hbm.1, bf16[2,2,4,256,256]{4,3,2,1,0:T(8,128)(2,1)} %w_hbm.1, bf16[2,2,4,256,256]{4,3,2,1,0:T(8,128)(2,1)} %r_hbm.1, bf16[2,4,256,256]{3,2,1,0:T(8,128)(2,1)} %t_hbm.1), custom_call_target="tpu_custom_call" | custom-call | tf_op jit(solution)/shard_map/born_step/pallas_call | solution.py:425
  130.6 4.6 %copy.6 = f32[2,2,4,256,256]{4,3,2,1,0:T(8,128)} copy(f32[2,2,4,256,256]{4,3,2,1,0:T(8,128)} %born_step.1) | data formatting | bytes 8388608

commit v3 on v2

--- a/solution.py
+++ b/solution.py
@@ -56,9 +56,12 @@
     return total
 
 
-def congruence(xh, xl, state, ih, il, exact=False):
-    high, low = split(state)
-    inner = product(xh, xl, high, None if exact else low)
+def congruence(xh, xl, state, ih, il, exact=False, brief=False):
+    high, low = (state.astype(BF16), None) if exact else split(state)
+    inner = product(xh, xl, high, low)
+    if brief:
+        put3(ih, inner.astype(BF16))
+        return right(ih, xh) + right(ih, xl)
     high, low = split(inner)
     put3(ih, high)
     put3(il, low)
@@ -67,7 +70,7 @@
 
 def kernel(
     g_hbm, w_hbm, r_hbm, t_hbm, out_hbm,
-    gbuf, wbuf, sig, smat, g3, coup, kh, kl, ph, pw, yh, yl, bst, cin,
+    gbuf, wbuf, sig, smat, g3, coup, kh, kl, ph, pw, yh, yl, wh, wl, bst, cin,
     mh, ml, nh, nl, arow, rrow, zh, zl, pre, ih, il, gf, wf,
     fs, fr, rs, rr, ms, mr, ns, nr, asend, arecv, xs, xr, ld, od,
 ):
@@ -217,23 +220,26 @@
                     sig[s, 0, n, rr_, cc_] = (im * (-1.0 / POINTS)).astype(BF16)
                     sig[s, 1, n, rr_, cc_] = (re * (1.0 / POINTS)).astype(BF16)
 
-    parts = (pl.ds(0, SLABS - 1), pl.ds(SLABS - 1, 1))
-
-    def giveback(e, part, k):
+    def giveback(e, s, k):
         p = (me + k) % PEERS
         return pltpu.make_async_remote_copy(
-            src_ref=sig.at[parts[part], :, 2 * p + e],
-            dst_ref=smat.at[e, parts[part], :, stripe(me)],
-            send_sem=rs.at[e, part, k],
-            recv_sem=rr.at[e, part, k],
+            src_ref=sig.at[s, :, 2 * p + e],
+            dst_ref=smat.at[e, s, :, stripe(me)],
+            send_sem=rs.at[e, s, k],
+            recv_sem=rr.at[e, s, k],
             device_id={"energy": p},
             device_id_type=MESH,
         )
 
-    def keep(e, part):
+    def keep(e, s):
         return pltpu.make_async_copy(
-            sig.at[parts[part], :, 2 * me + e], smat.at[e, parts[part], :, stripe(me)], rr.at[e, part, 0]
+            sig.at[s, :, 2 * me + e], smat.at[e, s, :, stripe(me)], rr.at[e, s, 0]
         )
+
+    def send_back(e, s):
+        for k in range(1, PEERS):
+            giveback(e, s, k).start()
+        keep(e, s).start()
 
     def row_products(e):
         for i in range(2):
@@ -250,55 +256,68 @@
 
         @pl.loop(0, SIDE)
         def _(j):
+            now = j % 2
+
+            @pl.when(j == z)
+            def _():
+                yh[e] = zh[now]
+                yl[e] = zl[now]
+
             mh[j, e, 0] = -mh[j, e, 2]
             ml[j, e, 0] = -ml[j, e, 2]
-            value = product(mh[j, e], ml[j, e], rows(zh[j, 1:3]), rows(zl[j, 1:3]))
+            value = product(mh[j, e], ml[j, e], rows(zh[now, 1:3]), rows(zl[now, 1:3]))
             high, low = split(value)
-            put3(zh.at[j + 1], high)
-            put3(zl.at[j + 1], low)
-
-        nh[x, e] = zh[SIDE]
-        nl[x, e] = zl[SIDE]
+            put3(zh.at[1 - now], high)
+            put3(zl.at[1 - now], low)
+
+        nh[x, e] = zh[0]
+        nl[x, e] = zl[0]
 
         @pl.when(x > 0)
         def _():
             for i in range(2):
                 upward(lambda k: send_n(e, k, i).start())
 
-        yh[e] = zh[z]
-        yl[e] = zl[z]
+        @pl.when(x < SIDE - 1)
+        def _():
+            wh[e, SIDE - 2] = mh[SIDE - 1, e]
+            wl[e, SIDE - 2] = ml[SIDE - 1, e]
+
+            @pl.loop(1, SIDE - 1)
+            def _(i):
+                j = SIDE - 2 - i
+                value = product(
+                    wh[e, j + 1], wl[e, j + 1], rows(mh[j + 1, e, 1:3]), rows(ml[j + 1, e, 1:3])
+                )
+                high, low = split(value)
+                put3(wh.at[e, j], high)
+                put3(wl.at[e, j], low)
 
     @pl.loop(0, SLABS - 2)
     def _(s):
         convolve(s)
+        send_back(0, s)
 
     row_products(0)
-    convolve(SLABS - 2)
-    for k in range(1, PEERS):
-        giveback(0, 0, k).start()
-    keep(0, 0).start()
-    convolve(SLABS - 1)
-    for e, part in ((0, 1), (1, 0), (1, 1)):
-        for k in range(1, PEERS):
-            giveback(e, part, k).start()
-        keep(e, part).start()
+
+    @pl.loop(SLABS - 2, SLABS)
+    def _(s):
+        convolve(s)
+        send_back(0, s)
+
+    @pl.loop(0, SLABS)
+    def _(s):
+        send_back(1, s)
+
     row_products(1)
-
-    def returned(e, part):
-        keep(e, part).wait()
-        for k in range(1, PEERS):
-            giveback(e, part, k).wait_recv()
 
     @pl.loop(0, EN)
     def _(e):
-        returned(e, 0)
-
         @pl.loop(0, SLABS)
         def _(s):
-            @pl.when(s == SLABS - 1)
-            def _():
-                returned(e, 1)
-
+            keep(e, s).wait()
+            for k in range(1, PEERS):
+                giveback(e, s, k).wait_recv()
             mixed = left(g3[e, s], smat[e, s, 0], smat[e, s, 1]).astype(BF16)
             put3(ih, mixed)
             bst[e, s] = right(ih, g3[e, s]).reshape(2, NORB, NORB)
@@ -312,38 +331,27 @@
         for k in (2, 1, 3):
             send_a(e, k).start()
 
-    top = jnp.where(x < SIDE - 1, SIDE, jnp.maximum(z, 1))
-
     @pl.loop(0, EN)
     def _(e):
-        def arrived(j):
-            k = (z - j + SIDE) % SIDE
+        pre[SIDE] = jnp.zeros((2, NORB, NORB), F32)
+
+        @pl.loop(0, SIDE)
+        def _(t):
+            k = jnp.where(t < 2, t, SIDE + 1 - t)
+            j = (z - k + SIDE) % SIDE
 
             @pl.when(k > 0)
             def _():
                 send_a(e, k).wait_recv()
 
-        def step(j, exact):
-            value = congruence(mh[j, e], ml[j, e], rows(pre[j]), ih, il, exact)
-            pre[j + 1] = value.reshape(2, NORB, NORB)
-            arrived(j)
-            pre[j + 1] += arow[j, e].astype(F32)
-
-        pre[0] = jnp.zeros((2, NORB, NORB), F32)
-        arrived(0)
-        pre[1] = arow[0, e].astype(F32)
-
-        @pl.when(top > 1)
-        def _():
-            step(1, True)
-
-            @pl.loop(2, top)
-            def _(j):
-                step(j, False)
-
-        @pl.loop(top, SIDE)
-        def _(j):
-            arrived(j)
+            @pl.when((x < SIDE - 1) & (j < SIDE - 1))
+            def _():
+                value = congruence(wh[e, j], wl[e, j], rows(arow[j, e]), ih, il, True)
+                pre[SIDE] += value.reshape(2, NORB, NORB)
+
+            @pl.when(j == SIDE - 1)
+            def _():
+                pre[SIDE] += arow[j, e].astype(F32)
 
         @pl.when(x < SIDE - 1)
         def _():
@@ -353,6 +361,14 @@
                 @pl.when(x + k < SIDE)
                 def _(k=k):
                     send_r(e, k).start()
+
+        pre[0] = jnp.zeros((2, NORB, NORB), F32)
+        pre[1] = arow[0, e].astype(F32)
+
+        @pl.loop(1, z)
+        def _(j):
+            value = congruence(mh[j, e], ml[j, e], rows(pre[j]), ih, il)
+            pre[j + 1] = value.reshape(2, NORB, NORB) + arow[j, e].astype(F32)
 
         cin[e] = pre[z]
 
@@ -391,7 +407,7 @@
         def _(s):
             @pl.when(slab > 0)
             def _():
-                value = congruence(ph[e, s], pw[e, s], rows(cin[e]), ih, il)
+                value = congruence(ph[e, s], pw[e, s], rows(cin[e]), ih, il, True, True)
                 bst[e, s] += value.reshape(2, NORB, NORB)
 
             store(e, s).start()
@@ -410,9 +426,9 @@
             for i in range(2):
                 upward(lambda k: send_n(e, k, i).wait_send())
 
-        for part in range(2):
+        for s in range(SLABS):
             for k in range(1, PEERS):
-                giveback(e, part, k).wait_send()
+                giveback(e, s, k).wait_send()
     for s in range(SLABS):
         for k in range(1, PEERS):
             for a in range(2):
@@ -440,6 +456,8 @@
             pltpu.VMEM((EN, SLABS, 3) + block, BF16),
             pltpu.VMEM((EN, 3) + block, BF16),
             pltpu.VMEM((EN, 3) + block, BF16),
+            pltpu.VMEM((EN, SIDE - 1, 3) + block, BF16),
+            pltpu.VMEM((EN, SIDE - 1, 3) + block, BF16),
             pltpu.VMEM((EN, SLABS, 2) + block, F32),
             pltpu.VMEM((EN, 2) + block, F32),
             pltpu.VMEM((SIDE, EN, 3) + block, BF16),
@@ -448,8 +466,8 @@
             pltpu.VMEM((SIDE, EN, 3) + block, BF16),
             pltpu.VMEM((SIDE, EN, 2) + block, BF16),
             pltpu.VMEM((SIDE, EN, 2) + block, BF16),
-            pltpu.VMEM((SIDE + 1, 3) + block, BF16),
-            pltpu.VMEM((SIDE + 1, 3) + block, BF16),
+            pltpu.VMEM((2, 3) + block, BF16),
+            pltpu.VMEM((2, 3) + block, BF16),
             pltpu.VMEM((SIDE + 1, 2) + block, F32),
             pltpu.VMEM((3,) + block, BF16),
             pltpu.VMEM((3,) + block, BF16),
@@ -457,8 +475,8 @@
             pltpu.VMEM((2, POINTS, 16, 128), F32),
             dma((2, SLABS, PEERS)),
             dma((2, SLABS, PEERS)),
-            dma((EN, 2, PEERS)),
-            dma((EN, 2, PEERS)),
+            dma((EN, SLABS, PEERS)),
+            dma((EN, SLABS, PEERS)),
             dma((2, EN, SIDE)),
             dma((2, EN, SIDE)),
             dma((2, EN, SIDE)),

time: 137 us -> 133 us (0.971); the launches traced: 135 us -> 133 us
  Pallas kernels: 131 us -> 129 us
    pallas_call x1, Pallas kernels: 131 us -> 129 us  [per_device(): pl.pallas_call(kernel, out_shape=jax.ShapeDtypeStruct((2, EN, SLABS) + bl...]
where the time goes in v3:
time: 133 us
  Pallas kernels  129 us (97%)
  local copies, waits for them, and re-layouts  4.6 us (3%)
    pallas_call x1, Pallas kernels, per_device(): pl.pallas_call(kernel, out_shape=jax.ShapeDtypeStruct((2, EN, SLABS) + bl...  129 us
    unnamed x1, local copies, waits for them, and re-layouts  4.6 us

profile of v3, /device:TPU:31, one launch (start us, length us, event | category | flops | bytes accessed | tf_op | source)
XLA Modules:
  0.0 133.3 jit_solution(14635009739060865673)
XLA Ops:
  0.0 128.7 %born_step.1 = f32[2,2,4,256,256]{4,3,2,1,0:T(8,128)} custom-call(bf16[2,2,4,256,256]{4,3,2,1,0:T(8,128)(2,1)} %g_hbm.1, bf16[2,2,4,256,256]{4,3,2,1,0:T(8,128)(2,1)} %w_hbm.1, bf16[2,2,4,256,256]{4,3,2,1,0:T(8,128)(2,1)} %r_hbm.1, bf16[2,4,256,256]{3,2,1,0:T(8,128)(2,1)} %t_hbm.1), custom_call_target="tpu_custom_call" | custom-call | tf_op jit(solution)/shard_map/born_step/pallas_call | solution.py:441
  128.7 4.6 %copy.6 = f32[2,2,4,256,256]{4,3,2,1,0:T(8,128)} copy(f32[2,2,4,256,256]{4,3,2,1,0:T(8,128)} %born_step.1) | data formatting | bytes 8388608

commit v4 on v3

--- a/solution.py
+++ b/solution.py
@@ -70,7 +70,7 @@
 
 def kernel(
     g_hbm, w_hbm, r_hbm, t_hbm, out_hbm,
-    gbuf, wbuf, sig, smat, g3, coup, kh, kl, ph, pw, yh, yl, wh, wl, bst, cin,
+    gbuf, wbuf, sig, smat, g3, coup, kh, kl, ph, pw, vh, vl, wh, wl, bst, cin,
     mh, ml, nh, nl, arow, rrow, zh, zl, pre, ih, il, gf, wf,
     fs, fr, rs, rr, ms, mr, ns, nr, asend, arecv, xs, xr, ld, od,
 ):
@@ -146,7 +146,7 @@
         return gather(k, view, view, ms.at[i, e, k], mr.at[i, e, k], z_peer(k))
 
     def send_n(e, k, i):
-        view = (nh, nl)[i].at[x, e, pl.ds(1, 2)]
+        view = (nh, nl)[i].at[x - 1, e]
         return gather(k, view, view, ns.at[i, e, k], nr.at[i, e, k], x_peer(k))
 
     def upward(act):
@@ -260,8 +260,9 @@
 
             @pl.when(j == z)
             def _():
-                yh[e] = zh[now]
-                yl[e] = zl[now]
+                first = jnp.maximum(x - 1, 0)
+                vh[e, first] = zh[now]
+                vl[e, first] = zl[now]
 
             mh[j, e, 0] = -mh[j, e, 2]
             ml[j, e, 0] = -ml[j, e, 2]
@@ -270,11 +271,10 @@
             put3(zh.at[1 - now], high)
             put3(zl.at[1 - now], low)
 
-        nh[x, e] = zh[0]
-        nl[x, e] = zl[0]
-
-        @pl.when(x > 0)
+        @pl.when((x > 0) & (x < SIDE - 1))
         def _():
+            nh[x - 1, e] = zh[0, 1:3]
+            nl[x - 1, e] = zl[0, 1:3]
             for i in range(2):
                 upward(lambda k: send_n(e, k, i).start())
 
@@ -333,6 +333,18 @@
 
     @pl.loop(0, EN)
     def _(e):
+        @pl.loop(1, x)
+        def _(i):
+            j = x - i
+            for part in range(2):
+                pltpu.make_async_copy(
+                    (nh, nl)[part].at[j - 1, e], (nh, nl)[part].at[j - 1, e], nr.at[part, e, x - j]
+                ).wait()
+            value = product(vh[e, j], vl[e, j], rows(nh[j - 1, e]), rows(nl[j - 1, e]))
+            high, low = split(value)
+            put3(vh.at[e, j - 1], high)
+            put3(vl.at[e, j - 1], low)
+
         pre[SIDE] = jnp.zeros((2, NORB, NORB), F32)
 
         @pl.loop(0, SIDE)
@@ -377,38 +389,24 @@
 
     @pl.loop(0, EN)
     def _(e):
-        def step(j, exact):
-            for i in range(2):
-                send_n(e, x - j, i).wait_recv()
-            nh[j, e, 0] = -nh[j, e, 2]
-            nl[j, e, 0] = -nl[j, e, 2]
-            value = congruence(nh[j, e], nl[j, e], rows(pre[j]), ih, il, exact)
-            pre[j + 1] = value.reshape(2, NORB, NORB)
-            send_r(e, x - j).wait_recv()
-            pre[j + 1] += rrow[j, e].astype(F32)
-
-        @pl.when(x > 0)
-        def _():
-            send_r(e, x).wait_recv()
-            pre[1] = rrow[0, e].astype(F32)
-
-            @pl.when(x > 1)
-            def _():
-                step(1, True)
-
-                @pl.loop(2, x)
-                def _(j):
-                    step(j, False)
-
-            value = congruence(yh[e], yl[e], rows(pre[x]), ih, il)
+        @pl.loop(0, x)
+        def _(t):
+            k = jnp.where(x < SIDE - 1, t + 1, jnp.where(t == 0, SIDE - 1, t))
+            j = x - k
+            send_r(e, k).wait_recv()
+            value = congruence(vh[e, j], vl[e, j], rows(rrow[j, e]), ih, il, True)
             cin[e] += value.reshape(2, NORB, NORB)
 
         @pl.loop(0, SLABS)
         def _(s):
+            @pl.when(slab == 0)
+            def _():
+                bst[e, s] = bst[e, s] * 0.5
+
             @pl.when(slab > 0)
             def _():
                 value = congruence(ph[e, s], pw[e, s], rows(cin[e]), ih, il, True, True)
-                bst[e, s] += value.reshape(2, NORB, NORB)
+                bst[e, s] = (bst[e, s] + value.reshape(2, NORB, NORB)) * 0.5
 
             store(e, s).start()
 
@@ -421,7 +419,7 @@
             send_a(e, k).wait_send()
         upward(lambda k: send_r(e, k).wait_send())
 
-        @pl.when(x > 0)
+        @pl.when((x > 0) & (x < SIDE - 1))
         def _(e=e):
             for i in range(2):
                 upward(lambda k: send_n(e, k, i).wait_send())
@@ -438,7 +436,7 @@
 def per_device(green_lesser, screened_lesser, green_retarded, coupling):
     block = (NORB, NORB)
     dma = pltpu.SemaphoreType.DMA
-    return pl.pallas_call(
+    half = pl.pallas_call(
         kernel,
         out_shape=jax.ShapeDtypeStruct((2, EN, SLABS) + block, F32),
         in_specs=[pl.BlockSpec(memory_space=pl.ANY)] * 4,
@@ -454,16 +452,16 @@
             pltpu.VMEM((EN, SLABS, 3) + block, BF16),
             pltpu.VMEM((EN, SLABS, 3) + block, BF16),
             pltpu.VMEM((EN, SLABS, 3) + block, BF16),
-            pltpu.VMEM((EN, 3) + block, BF16),
-            pltpu.VMEM((EN, 3) + block, BF16),
+            pltpu.VMEM((EN, SIDE - 1, 3) + block, BF16),
+            pltpu.VMEM((EN, SIDE - 1, 3) + block, BF16),
             pltpu.VMEM((EN, SIDE - 1, 3) + block, BF16),
             pltpu.VMEM((EN, SIDE - 1, 3) + block, BF16),
             pltpu.VMEM((EN, SLABS, 2) + block, F32),
             pltpu.VMEM((EN, 2) + block, F32),
             pltpu.VMEM((SIDE, EN, 3) + block, BF16),
             pltpu.VMEM((SIDE, EN, 3) + block, BF16),
-            pltpu.VMEM((SIDE, EN, 3) + block, BF16),
-            pltpu.VMEM((SIDE, EN, 3) + block, BF16),
+            pltpu.VMEM((SIDE - 2, EN, 2) + block, BF16),
+            pltpu.VMEM((SIDE - 2, EN, 2) + block, BF16),
             pltpu.VMEM((SIDE, EN, 2) + block, BF16),
             pltpu.VMEM((SIDE, EN, 2) + block, BF16),
             pltpu.VMEM((2, 3) + block, BF16),
@@ -493,6 +491,7 @@
         ),
         name="born_step",
     )(green_lesser, screened_lesser, green_retarded, coupling)
+    return half * 2.0
 
 
 def solution(mesh):

time: 133 us -> 131 us (0.985)
  local copies, waits for them, and re-layouts: 4.6 us -> 0 us
  other arithmetic: 0 us -> 4.54 us
  Pallas kernels: 129 us -> 126 us
    unnamed x1 -> x0, local copies, waits for them, and re-layouts: 4.6 us -> none
    mul x0 -> x1, other arithmetic: none -> 4.54 us  [per_device(): return half * 2.0]
    pallas_call x1, Pallas kernels: 129 us -> 126 us  [per_device(): pl.pallas_call(kernel, out_shape=jax.ShapeDtypeStruct((2, EN, SLABS) + bl...]
where the time goes in v4:
time: 131 us
  Pallas kernels  126 us (96%)
  other arithmetic  4.54 us (3%)
    pallas_call x1, Pallas kernels, per_device(): pl.pallas_call(kernel, out_shape=jax.ShapeDtypeStruct((2, EN, SLABS) + bl...  126 us
    mul x1, other arithmetic, per_device(): return half * 2.0  4.54 us

profile of v4, /device:TPU:31, one launch (start us, length us, event | category | flops | bytes accessed | tf_op | source)
XLA Modules:
  0.0 130.9 jit_solution(2589171652306131592)
XLA Ops:
  0.0 126.3 %born_step.1 = f32[2,2,4,256,256]{4,3,2,1,0:T(8,128)} custom-call(bf16[2,2,4,256,256]{4,3,2,1,0:T(8,128)(2,1)} %g_hbm.1, bf16[2,2,4,256,256]{4,3,2,1,0:T(8,128)(2,1)} %w_hbm.1, bf16[2,2,4,256,256]{4,3,2,1,0:T(8,128)(2,1)} %r_hbm.1, bf16[2,4,256,256]{3,2,1,0:T(8,128)(2,1)} %t_hbm.1), custom_call_target="tpu_custom_call" | custom-call | tf_op jit(solution)/shard_map/born_step/pallas_call | solution.py:439
  126.3 4.5 %broadcast_multiply_fusion = f32[2,2,4,256,256]{4,3,2,1,0:T(8,128)} fusion(f32[2,2,4,256,256]{4,3,2,1,0:T(8,128)} %born_step.1), kind=kLoop, calls=%fused_computation | loop fusion | flops 1048576 | bytes 8388608 | tf_op jit(solution)/shard_map/mul | solution.py:494

commit v5 on v4

--- a/solution.py
+++ b/solution.py
@@ -236,10 +236,14 @@
             sig.at[s, :, 2 * me + e], smat.at[e, s, :, stripe(me)], rr.at[e, s, 0]
         )
 
-    def send_back(e, s):
-        for k in range(1, PEERS):
-            giveback(e, s, k).start()
-        keep(e, s).start()
+    def send_back(e, s, core):
+        for d in (2, 1, 3, 0):
+            p = ((me // 2 + d) % SIDE) * 2 + core
+            k = (p - me + PEERS) % PEERS
+
+            @pl.when(k > 0)
+            def _(k=k):
+                giveback(e, s, k).start()
 
     def row_products(e):
         for i in range(2):
@@ -296,43 +300,28 @@
     @pl.loop(0, SLABS - 2)
     def _(s):
         convolve(s)
-        send_back(0, s)
+        send_back(0, s, 0)
+        for e in range(EN):
+            keep(e, s).start()
 
     row_products(0)
 
     @pl.loop(SLABS - 2, SLABS)
     def _(s):
         convolve(s)
-        send_back(0, s)
-
-    @pl.loop(0, SLABS)
-    def _(s):
-        send_back(1, s)
+        send_back(0, s, 0)
+        for e in range(EN):
+            keep(e, s).start()
+
+    for e, core in ((0, 1), (1, 0), (1, 1)):
+
+        @pl.loop(0, SLABS)
+        def _(s, e=e, core=core):
+            send_back(e, s, core)
 
     row_products(1)
 
-    @pl.loop(0, EN)
-    def _(e):
-        @pl.loop(0, SLABS)
-        def _(s):
-            keep(e, s).wait()
-            for k in range(1, PEERS):
-                giveback(e, s, k).wait_recv()
-            mixed = left(g3[e, s], smat[e, s, 0], smat[e, s, 1]).astype(BF16)
-            put3(ih, mixed)
-            bst[e, s] = right(ih, g3[e, s]).reshape(2, NORB, NORB)
-
-            @pl.when(s > 0)
-            def _():
-                value = congruence(kh[e, s], kl[e, s], rows(bst[e, s - 1]), ih, il)
-                bst[e, s] += value.reshape(2, NORB, NORB)
-
-        arow[z, e] = bst[e, SLABS - 1].astype(BF16)
-        for k in (2, 1, 3):
-            send_a(e, k).start()
-
-    @pl.loop(0, EN)
-    def _(e):
+    def row_windows(e):
         @pl.loop(1, x)
         def _(i):
             j = x - i
@@ -344,6 +333,34 @@
             high, low = split(value)
             put3(vh.at[e, j - 1], high)
             put3(vl.at[e, j - 1], low)
+
+    row_windows(0)
+
+    @pl.loop(0, EN)
+    def _(e):
+        @pl.loop(0, SLABS)
+        def _(s):
+            keep(e, s).wait()
+            for k in range(1, PEERS):
+                giveback(e, s, k).wait_recv()
+            mixed = left(g3[e, s], smat[e, s, 0], smat[e, s, 1]).astype(BF16)
+            put3(ih, mixed)
+            bst[e, s] = right(ih, g3[e, s]).reshape(2, NORB, NORB)
+
+            @pl.when(s > 0)
+            def _():
+                value = congruence(kh[e, s], kl[e, s], rows(bst[e, s - 1]), ih, il)
+                bst[e, s] += value.reshape(2, NORB, NORB)
+
+        arow[z, e] = bst[e, SLABS - 1].astype(BF16)
+        for k in (2, 1, 3):
+            send_a(e, k).start()
+
+    @pl.loop(0, EN)
+    def _(e):
+        @pl.when(e == 1)
+        def _():
+            row_windows(1)
 
         pre[SIDE] = jnp.zeros((2, NORB, NORB), F32)
 

time: 131 us -> 132 us (level)
  the two profiles are of different devices: /device:TPU:31 before, /device:TPU:39 now
where the time goes in v5:
time: 132 us
  Pallas kernels  127 us (96%)
  other arithmetic  4.54 us (3%)
    pallas_call x1, Pallas kernels, per_device(): pl.pallas_call(kernel, out_shape=jax.ShapeDtypeStruct((2, EN, SLABS) + bl...  127 us
    mul x1, other arithmetic, per_device(): return half * 2.0  4.54 us

profile of v5, /device:TPU:39, one launch (start us, length us, event | category | flops | bytes accessed | tf_op | source)
XLA Modules:
  0.0 131.8 jit_solution(15877199533648650735)
XLA Ops:
  0.0 127.2 %born_step.1 = f32[2,2,4,256,256]{4,3,2,1,0:T(8,128)} custom-call(bf16[2,2,4,256,256]{4,3,2,1,0:T(8,128)(2,1)} %g_hbm.1, bf16[2,2,4,256,256]{4,3,2,1,0:T(8,128)(2,1)} %w_hbm.1, bf16[2,2,4,256,256]{4,3,2,1,0:T(8,128)(2,1)} %r_hbm.1, bf16[2,4,256,256]{3,2,1,0:T(8,128)(2,1)} %t_hbm.1), custom_call_target="tpu_custom_call" | custom-call | tf_op jit(solution)/shard_map/born_step/pallas_call | solution.py:456
  127.2 4.5 %broadcast_multiply_fusion = f32[2,2,4,256,256]{4,3,2,1,0:T(8,128)} fusion(f32[2,2,4,256,256]{4,3,2,1,0:T(8,128)} %born_step.1), kind=kLoop, calls=%fused_computation | loop fusion | flops 1048576 | bytes 8388608 | tf_op jit(solution)/shard_map/mul | solution.py:511

commit v6 on v5

--- a/solution.py
+++ b/solution.py
@@ -236,14 +236,9 @@
             sig.at[s, :, 2 * me + e], smat.at[e, s, :, stripe(me)], rr.at[e, s, 0]
         )
 
-    def send_back(e, s, core):
-        for d in (2, 1, 3, 0):
-            p = ((me // 2 + d) % SIDE) * 2 + core
-            k = (p - me + PEERS) % PEERS
-
-            @pl.when(k > 0)
-            def _(k=k):
-                giveback(e, s, k).start()
+    def send_back(e, s):
+        for k in range(1, PEERS):
+            giveback(e, s, k).start()
 
     def row_products(e):
         for i in range(2):
@@ -300,7 +295,7 @@
     @pl.loop(0, SLABS - 2)
     def _(s):
         convolve(s)
-        send_back(0, s, 0)
+        send_back(0, s)
         for e in range(EN):
             keep(e, s).start()
 
@@ -309,15 +304,13 @@
     @pl.loop(SLABS - 2, SLABS)
     def _(s):
         convolve(s)
-        send_back(0, s, 0)
+        send_back(0, s)
         for e in range(EN):
             keep(e, s).start()
 
-    for e, core in ((0, 1), (1, 0), (1, 1)):
-
-        @pl.loop(0, SLABS)
-        def _(s, e=e, core=core):
-            send_back(e, s, core)
+    @pl.loop(0, SLABS)
+    def _(s):
+        send_back(1, s)
 
     row_products(1)
 
@@ -394,10 +387,15 @@
         pre[0] = jnp.zeros((2, NORB, NORB), F32)
         pre[1] = arow[0, e].astype(F32)
 
-        @pl.loop(1, z)
-        def _(j):
-            value = congruence(mh[j, e], ml[j, e], rows(pre[j]), ih, il)
-            pre[j + 1] = value.reshape(2, NORB, NORB) + arow[j, e].astype(F32)
+        @pl.when(z > 1)
+        def _():
+            value = congruence(mh[1, e], ml[1, e], rows(arow[0, e]), ih, il, True)
+            pre[2] = value.reshape(2, NORB, NORB) + arow[1, e].astype(F32)
+
+        @pl.when(z > 2)
+        def _():
+            value = congruence(mh[2, e], ml[2, e], rows(pre[2]), ih, il)
+            pre[3] = value.reshape(2, NORB, NORB) + arow[2, e].astype(F32)
 
         cin[e] = pre[z]
 
@@ -411,7 +409,7 @@
             k = jnp.where(x < SIDE - 1, t + 1, jnp.where(t == 0, SIDE - 1, t))
             j = x - k
             send_r(e, k).wait_recv()
-            value = congruence(vh[e, j], vl[e, j], rows(rrow[j, e]), ih, il, True)
+            value = congruence(vh[e, j], vl[e, j], rows(rrow[j, e]), ih, il, True, True)
             cin[e] += value.reshape(2, NORB, NORB)
 
         @pl.loop(0, SLABS)

time: 132 us -> 131 us (level)
  the two profiles are of different devices: /device:TPU:39 before, /device:TPU:31 now
where the time goes in v6:
time: 131 us
  Pallas kernels  126 us (96%)
  other arithmetic  4.54 us (3%)
    pallas_call x1, Pallas kernels, per_device(): pl.pallas_call(kernel, out_shape=jax.ShapeDtypeStruct((2, EN, SLABS) + bl...  126 us
    mul x1, other arithmetic, per_device(): return half * 2.0  4.54 us

profile of v6, /device:TPU:31, one launch (start us, length us, event | category | flops | bytes accessed | tf_op | source)
XLA Modules:
  0.0 130.9 jit_solution(12163095237398480082)
XLA Ops:
  0.0 126.4 %born_step.1 = f32[2,2,4,256,256]{4,3,2,1,0:T(8,128)} custom-call(bf16[2,2,4,256,256]{4,3,2,1,0:T(8,128)(2,1)} %g_hbm.1, bf16[2,2,4,256,256]{4,3,2,1,0:T(8,128)(2,1)} %w_hbm.1, bf16[2,2,4,256,256]{4,3,2,1,0:T(8,128)(2,1)} %r_hbm.1, bf16[2,4,256,256]{3,2,1,0:T(8,128)(2,1)} %t_hbm.1), custom_call_target="tpu_custom_call" | custom-call | tf_op jit(solution)/shard_map/born_step/pallas_call | solution.py:454
  126.4 4.5 %broadcast_multiply_fusion = f32[2,2,4,256,256]{4,3,2,1,0:T(8,128)} fusion(f32[2,2,4,256,256]{4,3,2,1,0:T(8,128)} %born_step.1), kind=kLoop, calls=%fused_computation | loop fusion | flops 1048576 | bytes 8388608 | tf_op jit(solution)/shard_map/mul | solution.py:509

commit v7 on v6

--- a/solution.py
+++ b/solution.py
@@ -346,7 +346,7 @@
                 bst[e, s] += value.reshape(2, NORB, NORB)
 
         arow[z, e] = bst[e, SLABS - 1].astype(BF16)
-        for k in (2, 1, 3):
+        for k in (1, 3, 2):
             send_a(e, k).start()
 
     @pl.loop(0, EN)
@@ -409,7 +409,7 @@
             k = jnp.where(x < SIDE - 1, t + 1, jnp.where(t == 0, SIDE - 1, t))
             j = x - k
             send_r(e, k).wait_recv()
-            value = congruence(vh[e, j], vl[e, j], rows(rrow[j, e]), ih, il, True, True)
+            value = congruence(vh[e, j], vl[e, j], rows(rrow[j, e]), ih, il, True)
             cin[e] += value.reshape(2, NORB, NORB)
 
         @pl.loop(0, SLABS)

time: 131 us -> 128 us (0.977)
  the two profiles are of different devices: /device:TPU:31 before, /device:TPU:102 now
where the time goes in v7:
time: 128 us
  Pallas kernels  124 us (97%)
  other arithmetic  4.54 us (4%)
    pallas_call x1, Pallas kernels, per_device(): pl.pallas_call(kernel, out_shape=jax.ShapeDtypeStruct((2, EN, SLABS) + bl...  124 us
    mul x1, other arithmetic, per_device(): return half * 2.0  4.54 us

profile of v7, /device:TPU:102, one launch (start us, length us, event | category | flops | bytes accessed | tf_op | source)
XLA Modules:
  0.0 128.3 jit_solution(3103043285773739977)
XLA Ops:
  0.0 123.7 %born_step.1 = f32[2,2,4,256,256]{4,3,2,1,0:T(8,128)} custom-call(bf16[2,2,4,256,256]{4,3,2,1,0:T(8,128)(2,1)} %g_hbm.1, bf16[2,2,4,256,256]{4,3,2,1,0:T(8,128)(2,1)} %w_hbm.1, bf16[2,2,4,256,256]{4,3,2,1,0:T(8,128)(2,1)} %r_hbm.1, bf16[2,4,256,256]{3,2,1,0:T(8,128)(2,1)} %t_hbm.1), custom_call_target="tpu_custom_call" | custom-call | tf_op jit(solution)/shard_map/born_step/pallas_call | solution.py:454
  123.8 4.5 %broadcast_multiply_fusion = f32[2,2,4,256,256]{4,3,2,1,0:T(8,128)} fusion(f32[2,2,4,256,256]{4,3,2,1,0:T(8,128)} %born_step.1), kind=kLoop, calls=%fused_computation | loop fusion | flops 1048576 | bytes 8388608 | tf_op jit(solution)/shard_map/mul | solution.py:509
